TPU v7x, 32 devices: a whole 2x2x4 slice. The times are simulated.
32 devices in a mesh: cfg: 2 (over core), tm: 2 (over x), space: 8 (over z, y).
Axes of the slice: x: 2, y: 2, z: 4, core: 2. Of those that a mesh axis runs over, the one named last changes fastest.
Arguments:
- solutions: bfloat16 [4, 2, 3, 1024, 384], P(('cfg', 'tm'), None, None, 'space'), parts along dimension 0, may hold values from -6 to 6
- eigvecs: bfloat16 [4, 2, 3, 1024, 384], P(('cfg', 'tm'), None, None, 'space'), parts along dimension 0, may hold values from -0.078125 to 0.078125
- meson: bfloat16 [4, 4, 2, 384, 384], P(None, ('cfg', 'tm')), parts along dimension 1, may hold values from -0.015625 to 0.015625
- momenta: int32 [4, 3], replicated, may hold values from -3 to 3
- source_time: int32 [384], replicated, may hold values from 0 to 1
- dilution: int32 [384], replicated, may hold values from 0 to 3
Outputs:
- blocks: float32 [4, 2, 384, 4, 384], P(None, None, ('tm', 'space'), 'cfg'), parts along dimension 3
There are 2 independent parts, one for each index of `cfg`. A program takes and returns all parts, laid end to end along the dimension named above; an argument that names none is the same for every part. Nothing has to cross between parts.
All inputs are finite; a program needn't handle non-finite values.
Results may differ from a plain program's by a relative error of at most 0.0056.
Values may be sent and summed in bfloat16 or wider, within the bound.
A program may use at most 64 MiB of HBM per device.

v0:
```python
import jax
import jax.numpy as jnp
from jax import lax
from jax.sharding import PartitionSpec as P

SIDE = 48
NDIL = 4


def contract(first_op, second_op):
    return lax.dot_general(
        first_op, second_op, (((1,), (1,)), ((0,), (0,))), preferred_element_type=jnp.float32
    )


def regroup(array, time_count, space_count, cols_local):
    leading = array.shape[:-1]
    split = array.reshape(leading + (time_count, space_count, cols_local))
    return jnp.swapaxes(split, -3, -2).reshape(leading + (time_count * space_count * cols_local,))


def ungroup(array, time_count, space_count, cols_local):
    leading = array.shape[:-1]
    split = array.reshape(leading + (space_count, time_count, cols_local))
    return jnp.swapaxes(split, -3, -2).reshape(leading + (time_count * space_count * cols_local,))


def project(stack_real, stack_imag, vec_real, vec_imag, set_count, amount):
    real_part = contract(stack_real, vec_real) + contract(stack_imag, vec_imag)
    imag_part = contract(stack_imag, vec_real) - contract(stack_real, vec_imag)
    stacked = jnp.stack([real_part, imag_part], 2)
    times_local = stacked.shape[0]
    stacked = stacked.reshape(times_local, amount, set_count, 2, stacked.shape[-1])
    return jnp.transpose(stacked, (1, 0, 2, 3, 4))


def momentum_blocks(momentum, meson):
    coef_real = momentum[:, :, :, 0]
    coef_imag = momentum[:, :, :, 1]
    meson_real = meson[:, :, 0]
    meson_imag = meson[:, :, 1]
    left_real = jnp.einsum(
        "atpk,ptkl->ptal", coef_real, meson_real, preferred_element_type=jnp.float32
    ) + jnp.einsum("atpk,ptkl->ptal", coef_imag, meson_imag, preferred_element_type=jnp.float32)
    left_imag = jnp.einsum(
        "atpk,ptkl->ptal", coef_real, meson_imag, preferred_element_type=jnp.float32
    ) - jnp.einsum("atpk,ptkl->ptal", coef_imag, meson_real, preferred_element_type=jnp.float32)
    return (left_real.astype(jnp.bfloat16), left_imag.astype(jnp.bfloat16))


def meson_block(portion, patterns_all, left_real, left_imag):
    vectors = portion.shape[-1]
    dilution_mask = (
        (jnp.arange(vectors, dtype=jnp.int32) % NDIL)[None, :] == patterns_all[:, None]
    ).astype(jnp.bfloat16)
    zero_mom = portion * dilution_mask[:, None, None, :]
    zero_real = zero_mom[:, :, 0]
    zero_imag = zero_mom[:, :, 1]
    real_part = jnp.einsum(
        "ptal,btl->tapb", left_real, zero_real, preferred_element_type=jnp.float32
    ) - jnp.einsum("ptal,btl->tapb", left_imag, zero_imag, preferred_element_type=jnp.float32)
    imag_part = jnp.einsum(
        "ptal,btl->tapb", left_real, zero_imag, preferred_element_type=jnp.float32
    ) + jnp.einsum("ptal,btl->tapb", left_imag, zero_real, preferred_element_type=jnp.float32)
    return jnp.stack([real_part, imag_part], 3)


def body(solutions, eigvecs, meson, momenta, source_time, dilution):
    times_local, _, colors, sites_local, columns = solutions.shape
    vectors = eigvecs.shape[4]
    moments = momenta.shape[0]
    space_count = lax.axis_size("space")
    time_count = lax.axis_size("tm")
    rows_local = columns // space_count
    cols_local = columns // (space_count * time_count)
    times_total = times_local * time_count
    grouped = regroup(solutions, time_count, space_count, cols_local)
    patterns_all = regroup(dilution, time_count, space_count, cols_local)
    site_index = lax.axis_index("space") * sites_local + jnp.arange(sites_local, dtype=jnp.int32)
    coordinates = jnp.stack(
        [site_index % SIDE, site_index // SIDE % SIDE, site_index // (SIDE * SIDE)], 0
    )
    windings = jnp.sum(momenta[:, :, None] * coordinates[None], 1)
    angles = 2.0 * jnp.pi / SIDE * windings.astype(jnp.float32)
    cosine = jnp.cos(angles)[:, None, None, :, None]
    sine_part = jnp.sin(angles)[:, None, None, :, None]
    solve_real = grouped[:, 0].astype(jnp.float32)
    solve_imag = grouped[:, 1].astype(jnp.float32)
    phased_real = cosine * solve_real[None] + sine_part * solve_imag[None]
    phased_imag = cosine * solve_imag[None] - sine_part * solve_real[None]
    flat_rows = colors * sites_local
    phased_real = (
        jnp.moveaxis(phased_real, 0, -1)
        .reshape(times_local, flat_rows, columns * moments)
        .astype(jnp.bfloat16)
    )
    phased_imag = (
        jnp.moveaxis(phased_imag, 0, -1)
        .reshape(times_local, flat_rows, columns * moments)
        .astype(jnp.bfloat16)
    )
    base_real = grouped[:, 0].reshape(times_local, flat_rows, columns)
    base_imag = grouped[:, 1].reshape(times_local, flat_rows, columns)
    vec_real = eigvecs[:, 0].reshape(times_local, flat_rows, vectors)
    vec_imag = eigvecs[:, 1].reshape(times_local, flat_rows, vectors)
    zero_terms = project(base_real, base_imag, vec_real, vec_imag, 1, columns)
    zero_all = lax.psum(zero_terms, "space").astype(jnp.bfloat16)[:, :, 0]
    momentum = lax.psum_scatter(
        project(
            phased_real,
            phased_imag,
            vec_real,
            vec_imag,
            moments,
            rows_local * lax.axis_size("space"),
        ),
        "space",
        scatter_dimension=0,
        tiled=True,
    ).astype(jnp.bfloat16)
    left_real, left_imag = momentum_blocks(momentum, meson)
    blocks = meson_block(zero_all, patterns_all, left_real, left_imag)
    outgoing = blocks.reshape(times_local, time_count, cols_local, moments, 2, columns)
    first_row = (lax.axis_index("tm") * space_count + lax.axis_index("space")) * cols_local
    my_sources = lax.dynamic_slice_in_dim(source_time, first_row, cols_local)
    offsets = (
        my_sources[:, None] + jnp.arange(times_total, dtype=jnp.int32)[None, :]
    ) % times_total
    selector = (
        offsets[:, :, None] == jnp.arange(times_total, dtype=jnp.int32)[None, None, :]
    ).astype(jnp.float32)
    received = lax.all_to_all(
        outgoing.astype(jnp.bfloat16), "tm", split_axis=1, concat_axis=0, tiled=True
    ).astype(outgoing.dtype)
    by_time = received.reshape(times_total, cols_local, received.shape[3], 2, columns)
    by_time = ungroup(by_time, time_count, space_count, cols_local)
    return jnp.einsum("adt,taprb->pradb", selector, by_time, precision=lax.Precision.HIGHEST)


def solution(mesh):
    return jax.shard_map(
        body,
        mesh=mesh,
        in_specs=(
            P(("cfg", "tm"), None, None, "space", None),
            P(("cfg", "tm"), None, None, "space", None),
            P(None, ("cfg", "tm"), None, None, None),
            P(),
            P(),
            P(),
        ),
        out_specs=P(None, None, ("tm", "space"), "cfg", None),
        check_vma=False,
    )
```

profile of v0, /device:TPU:0, one launch (start us, length us, event | category | flops | bytes accessed | tf_op | source)
XLA Modules:
  0.0 181.8 jit_solution(11664704982364159849)
XLA Ops:
  6.5 0.0 reduce-scatter.2.cloned.1.call-start
  6.6 0.8 copy.53
  7.4 0.1 multiply_reduce_fusion
  7.5 1.4 copy.50
  8.9 0.1 copy.51
  8.9 0.0 copy-start.3
  8.9 0.1 fusion.46
  9.0 0.4 copy.54
  9.4 0.4 copy.55
  9.9 0.1 copy-done.3
  10.0 0.1 fusion.65
  10.1 0.0 copy-start.4
  10.1 1.7 add_convert_fusion
  11.8 0.9 fusion.8
  12.6 2.3 %fusion.4 = f32[1536,384]{1,0:T(8,128)} fusion(bf16[384,384]{1,0:T(8,128)(2,1)S(1)} %bitcast.165, bf16[192,8,3,128]{3,2,1,0:T(4,128)(2,1)S(1)} %bitcast.154), kind=kOutput, calls=%fused_computation.15 | convolution fusion | flops 452984832 | bytes 3833856 | tf_op jit(solution)/shard_map/dot_general | solution.py:11
  14.9 0.0 copy-done.4
  14.9 2.3 %convolution_add_fusion = f32[1536,384]{1,0:T(8,128)} fusion(f32[1536,384]{1,0:T(8,128)S(1)} %fusion.8, bf16[384,384]{1,0:T(8,128)(2,1)S(1)} %bitcast.162, bf16[192,8,3,128]{3,2,1,0:T(4,128)(2,1)S(1)} %bitcast.155), kind=kOutput, calls=%fused_computation.4 | convolution fusion | flops 453574656 | bytes 6193152 | tf_op jit(solution)/shard_map/dot_general | solution.py:11
  17.3 3.6 %stack.37 = f32[384,1,4,1,384]{4,2,0,3,1:T(4,128)} reshape(f32[1536,384]{1,0:T(8,128)} %convolution_add_fusion) | data formatting | bytes 4718592 | tf_op jit(solution)/shard_map/stack | solution.py:31
  20.8 0.0 copy-start
  20.9 0.0 copy-start.5
  20.9 3.4 %copy.56 = f32[384,1,4,1,384]{4,0,2,3,1:T(8,128)} copy(f32[384,1,4,1,384]{4,2,0,3,1:T(4,128)} %stack.37) | data formatting | bytes 4718592 | tf_op jit(solution)/shard_map/stack | solution.py:31
  24.2 0.0 copy-done
  24.2 0.0 copy-done.5
  24.2 2.3 %convolution_subtract_fusion = f32[1536,384]{1,0:T(8,128)} fusion(f32[1536,384]{1,0:T(8,128)S(1)} %copy-done, bf16[384,384]{1,0:T(8,128)(2,1)S(1)} %bitcast.163, bf16[192,8,3,128]{3,2,1,0:T(4,128)(2,1)S(1)} %bitcast.153), kind=kOutput, calls=%fused_computation.3 | convolution fusion | flops 453574656 | bytes 6193152 | tf_op jit(solution)/shard_map/dot_general | solution.py:11
  26.6 2.6 %stack.38 = f32[384,1,4,1,384]{4,2,0,3,1:T(4,128)S(1)} reshape(f32[1536,384]{1,0:T(8,128)} %convolution_subtract_fusion) | data formatting | bytes 4718592 | tf_op jit(solution)/shard_map/stack | solution.py:31
  29.2 0.0 copy-start.2
  29.2 0.2 copy.57
  29.4 1.5 copy-done.2
  30.9 2.4 %pad_maximum_fusion = f32[384,1,4,2,384]{4,0,2,3,1:T(8,128)} fusion(f32[384,1,4,1,384]{4,0,2,3,1:T(8,128)S(1)} %copy.57, f32[384,1,4,1,384]{4,0,2,3,1:T(8,128)S(1)} %copy-done.2), kind=kLoop, calls=%fused_computation | loop fusion | flops 1179648 | bytes 9437184 | tf_op jit(solution)/shard_map/stack | solution.py:31
  33.3 0.0 reduce-scatter.2.cloned.1.call-update
  33.3 0.3 convolution_bitcast_fusion.3
  33.7 0.3 convolution_bitcast_fusion.1
  34.0 0.3 fusion.1
  34.3 0.0 copy-start.6
  34.4 0.3 fusion.3
  34.7 0.1 maximum_bitcast_fusion
  34.8 0.2 copy-done.6
  35.0 0.0 copy-start.1
  35.0 0.1 reshape.419
  35.1 0.1 eq.40
  35.2 0.9 dynamic_slice.3
  36.1 0.9 compare_convert_fusion
  37.0 92.2 %all-reduce.1 = bf16[384,1,1,2,384]{4,0,3,2,1:T(8,128)(2,1)} all-reduce(f32[384,1,1,2,384]{4,0,3,2,1:T(8,128)S(1)} %maximum_bitcast_fusion), channel_id=1, replica_groups=mesh['cfg'=2,'tm'=2,'space'=8] {'space'}, use_global_device_ids=true, to_apply=%region_0.1 | all-reduce | flops 294912 | bytes 1769472 | tf_op jit(solution)/shard_map/psum | solution.py:107
  129.2 1.2 bitcast_multiply_fusion
  130.4 25.2 %reduce-scatter.2.cloned.1.call-done = f32[48,1,4,2,384]{4,0,2,3,1:T(8,128)} async-done(((f32[384,1,4,2,384]{4,0,2,3,1:T(8,128)}), f32[48,1,4,2,384]{4,0,2,3,1:T(8,128)}) %reduce-scatter.2.cloned.1.call-update) | async-done | bytes 589840 | tf_op jit(solution)/shard_map/reduce_scatter | solution.py:108
  155.6 1.1 convert_element_type.87
  156.7 0.0 copy-done.1
  156.7 0.3 fusion.12
  157.0 0.3 fusion.10
  157.3 0.3 fusion.29
  157.6 0.3 fusion.44
  157.9 0.3 fusion.45
  158.1 0.3 fusion.26
  158.4 0.3 fusion.24
  158.7 0.3 fusion.25
  159.0 0.7 copy.65
  159.8 3.6 %all-to-all-start = ((bf16[1,2,24,4,2,384]{5,2,3,4,0,1:T(8,128)(2,1)}), bf16[1,2,24,4,2,384]{5,2,3,4,0,1:T(8,128)(2,1)S(1)}, u32[]{:S(2)}, u32[]{:S(2)}) async-start(bf16[1,2,24,4,2,384]{5,2,3,4,0,1:T(8,128)(2,1)} %copy.65), calls=%async_computation.1 | async-start | bytes 589824 | tf_op jit(solution)/shard_map/all_to_all | solution.py:132
  163.4 0.1 add_select_fusion
  163.5 5.2 %all-to-all-done = bf16[1,2,24,4,2,384]{5,2,3,4,0,1:T(8,128)(2,1)S(1)} async-done(((bf16[1,2,24,4,2,384]{5,2,3,4,0,1:T(8,128)(2,1)}), bf16[1,2,24,4,2,384]{5,2,3,4,0,1:T(8,128)(2,1)S(1)}, u32[]{:S(2)}, u32[]{:S(2)}) %all-to-all-start) | async-done | bytes 294944 | tf_op jit(solution)/shard_map/all_to_all | solution.py:132
  168.7 2.0 %reshape_reshape.3 = bf16[2,24,4,2,8,2,24]{6,5,4,1,2,3,0:T(2,128)(2,1)S(1)} reshape(bf16[1,2,24,4,2,384]{5,2,3,4,0,1:T(8,128)(2,1)S(1)} %all-to-all-done) | data formatting | bytes 589824 | tf_op jit(solution)/shard_map/reshape;reshape | solution.py:24
  170.7 0.4 copy.87
  171.2 2.2 %reshape.428 = bf16[2,24,4,2,384]{4,0,3,2,1:T(2,128)(2,1)S(1)} reshape(bf16[2,24,4,2,2,8,24]{6,5,4,0,3,2,1:T(8,128)(2,1)S(1)} %bitcast.161) | data formatting | bytes 589824 | tf_op jit(solution)/shard_map/reshape | solution.py:25
  173.4 0.5 convolution_bitcast_fusion
  173.9 1.0 copy.63
  (7 shorter events, 0.1 us)
Async XLA Ops:
  6.5 149.1 %reduce-scatter.2.cloned.1.call-start = ((), (), s32[]{:S(2)}) async-start(), calls=%async_computation.2 | async-start | bytes 5308416 | tf_op jit(solution)/shard_map/reduce_scatter | solution.py:108
  8.9 1.1 copy-start.3
  10.1 4.9 %copy-start.4 = (bf16[1,1,3,128,384]{4,3,2,1,0:T(8,128)(2,1)}, bf16[1,1,3,128,384]{4,3,2,1,0:T(8,128)(2,1)S(1)}, u32[]{:S(2)}) copy-start(bf16[1,1,3,128,384]{4,3,2,1,0:T(8,128)(2,1)S(1)} %get-tuple-element.7) | copy-start | bytes 884740
  20.8 3.4 %copy-start = (f32[1536,384]{1,0:T(8,128)S(1)}, f32[1536,384]{1,0:T(8,128)}, u32[]{:S(2)}) copy-start(f32[1536,384]{1,0:T(8,128)} %fusion.4) | copy-start | bytes 7077892
  20.9 3.4 %copy-start.5 = (bf16[1,1,3,128,384]{4,3,2,1,0:T(8,128)(2,1)S(1)}, bf16[1,1,3,128,384]{4,3,2,1,0:T(8,128)(2,1)}, u32[]{:S(2)}) copy-start(bf16[1,1,3,128,384]{4,3,2,1,0:T(8,128)(2,1)} %copy-done.4) | copy-start | bytes 884740
  29.2 1.7 copy-start.2
  34.3 0.7 copy-start.6
  35.0 121.7 %copy-start.1 = (bf16[4,1,2,384,384]{4,3,2,1,0:T(8,128)(2,1)S(1)}, bf16[4,1,2,384,384]{4,3,2,1,0:T(8,128)(2,1)}, u32[]{:S(2)}) copy-start(bf16[4,1,2,384,384]{4,3,2,1,0:T(8,128)(2,1)} %param.8) | copy-start | bytes 7077892
  159.8 9.0 %all-to-all-start = ((bf16[1,2,24,4,2,384]{5,2,3,4,0,1:T(8,128)(2,1)}), bf16[1,2,24,4,2,384]{5,2,3,4,0,1:T(8,128)(2,1)S(1)}, u32[]{:S(2)}, u32[]{:S(2)}) async-start(bf16[1,2,24,4,2,384]{5,2,3,4,0,1:T(8,128)(2,1)} %copy.65), calls=%async_computation.1 | async-start | bytes 589824 | tf_op jit(solution)/shard_map/all_to_all | solution.py:132
Sparse Core Ops, SparseCore 0:
  33.4 122.1 reduce-scatter.1
where the time goes:
time: 182 us
  blocking collectives  92.2 us (51%)
  waiting for transfers between devices  30.5 us (17%)
  local copies, waits for them, and re-layouts  22.2 us (12%)
  between operations  13.7 us (8%)
  matrix products  11.9 us (7%)
  other arithmetic  7.73 us (4%)
  starting transfers between devices  3.63 us (2%)
    psum x1, blocking collectives, body(): zero_all = lax.psum(zero_terms, 'space').astype(jnp.bfloat16)[:, :, 0]  92.2 us
    reduce_scatter x1, waiting for transfers between devices, body(): lax.psum_scatter(project(phased_real, phased_imag, vec_real, vec_imag, mo...  25.2 us
    another operation x4, local copies, waits for them, and re-layouts, project(): stacked = jnp.stack([real_part, imag_part], 2)  9.73 us
    dot_general x8, matrix products, contract(): lax.dot_general(first_op, second_op, (((1,), (1,)), ((0,), (0,))), prefer...  9.17 us
    all_to_all x1, waiting for transfers between devices, body(): lax.all_to_all(outgoing.astype(jnp.bfloat16), 'tm', split_axis=1, concat_...  5.24 us
    unnamed x16, local copies, waits for them, and re-layouts  4.05 us
  transfers between devices with their start and end apart: 2, of which 2 were waited for; matrix products, arithmetic and copies ran while one was open for 3% of the time, Pallas kernels for 0%

commit v1 on v0

v1 whole, which is shorter than its diff:
```python
import functools

import jax
import jax.numpy as jnp
import numpy as np
from jax import lax
from jax.experimental import pallas as pl
from jax.experimental.pallas import tpu as pltpu
from jax.sharding import PartitionSpec as P

SIDE = 48
NDIL = 4
MESH = pl.DeviceIdType.MESH
F32 = jnp.float32
BF16 = jnp.bfloat16


def dot(a, b, dims=((1,), (0,))):
    return lax.dot_general(a, b, (dims, ((), ())), preferred_element_type=F32)


def kernel(
    zc, tc,
    sol_ref, eig_ref, meson_hbm, cos_ref, sin_ref, dst_ref, dil_ref,
    out_ref,
    meson, solt, lhs, ysend, yrecv, own, zsend, zrecv, osend,
    q_y, q_yr, q_z, q_zr, q_f, q_fr, zfull, xrecv,
    meson_sem, ys, yr, zs, zr, xs, xr, qys, qyr, qzs, qzr, qfs, qfr,
):
    moments = cos_ref.shape[0]
    depth, cols = sol_ref.shape
    vecs = eig_ref.shape[1]
    half = cols // 2
    flat = depth // 2
    chunk = half // zc
    cl = chunk // tc
    small = vecs // NDIL

    s = lax.axis_index("space")
    t = lax.axis_index("tm")
    y = s % 2
    z = s // 2
    ypeer = {"space": z * 2 + (1 - y)}

    def zpeer(i):
        return {"space": ((z + i) % zc) * 2 + y}

    def xpeer(i):
        return (t + i) % tc

    def y_copy(p):
        return pltpu.make_async_remote_copy(
            src_ref=ysend.at[p], dst_ref=yrecv.at[p], send_sem=ys.at[p], recv_sem=yr.at[p],
            device_id=ypeer, device_id_type=MESH)

    def z_copy(p, i):
        return pltpu.make_async_remote_copy(
            src_ref=zsend.at[p, (z + i) % zc], dst_ref=zrecv.at[p, i - 1],
            send_sem=zs.at[p, i - 1], recv_sem=zr.at[p, i - 1],
            device_id=zpeer(i), device_id_type=MESH)

    def x_copy(p, i):
        return pltpu.make_async_remote_copy(
            src_ref=osend.at[p, xpeer(i)], dst_ref=xrecv.at[p, t],
            send_sem=xs.at[p, i - 1], recv_sem=xr.at[p, i - 1],
            device_id={"tm": xpeer(i)}, device_id_type=MESH)

    def qy_copy():
        return pltpu.make_async_remote_copy(
            src_ref=q_y.at[1 - y], dst_ref=q_yr, send_sem=qys, recv_sem=qyr,
            device_id=ypeer, device_id_type=MESH)

    def qz_copy(i):
        return pltpu.make_async_remote_copy(
            src_ref=q_z, dst_ref=q_zr.at[i - 1], send_sem=qzs.at[i - 1], recv_sem=qzr.at[i - 1],
            device_id=zpeer(i), device_id_type=MESH)

    def qf_copy():
        return pltpu.make_async_remote_copy(
            src_ref=q_f, dst_ref=q_fr, send_sem=qfs, recv_sem=qfr,
            device_id=ypeer, device_id_type=MESH)

    meson_copy = pltpu.make_async_copy(meson_hbm, meson, meson_sem)
    meson_copy.start()

    barrier = pltpu.get_barrier_semaphore()
    pl.semaphore_signal(barrier, inc=1, device_id=ypeer, device_id_type=MESH)
    for i in range(1, zc):
        pl.semaphore_signal(barrier, inc=1, device_id=zpeer(i), device_id_type=MESH)
    for i in range(1, tc):
        pl.semaphore_signal(barrier, inc=1, device_id={"tm": xpeer(i)}, device_id_type=MESH)

    sol = sol_ref[...]
    eig = eig_ref[...]
    turned = jnp.concatenate([sol[flat:], -sol[:flat]], 0)
    k_row = lax.broadcasted_iota(jnp.int32, (vecs, cols), 0)
    keep = (k_row & (NDIL - 1)) == dil_ref[...]
    j_row = lax.broadcasted_iota(jnp.int32, (small, vecs), 0) * NDIL
    k_col = lax.broadcasted_iota(jnp.int32, (small, vecs), 1)
    gather = ((k_col >= j_row) & (k_col < j_row + NDIL)).astype(F32).astype(BF16)
    for part, rhs in enumerate((sol, turned)):
        full = dot(eig, rhs, ((0,), (0,)))
        full = jnp.where(keep, full, 0.0).astype(BF16)
        q_y[part] = dot(gather, full).astype(BF16)

    c_row = lax.broadcasted_iota(jnp.int32, (cols, cols), 0)
    perm = (c_row == dst_ref[...]).astype(F32).astype(BF16)
    moved = dot(perm, sol, ((1,), (1,)))
    solt[0] = moved[:half]
    solt[1] = moved[half:]

    pl.semaphore_wait(barrier, 1 + (zc - 1) + (tc - 1))
    qy_copy().start()

    def partial(p, which):
        block = solt[which]
        re, im = block[:, :flat], block[:, flat:]
        c, sn = cos_ref[p], sin_ref[p]
        pr = (c * re + sn * im).astype(BF16)
        pi = (c * im - sn * re).astype(BF16)
        lhs[:half, :flat] = pr
        lhs[:half, flat:] = pi
        lhs[half:, :flat] = pi
        lhs[half:, flat:] = -pr
        return dot(lhs[...], eig_ref[...])

    def send_other(p, carry):
        ysend[p] = partial(p, 1 - y).astype(BF16)
        y_copy(p).start()
        return carry

    lax.fori_loop(0, moments, send_other, 0)

    qy_copy().wait_recv()
    q_z[...] = (q_y[y].astype(F32) + q_yr[...].astype(F32)).astype(BF16)
    for i in range(1, zc):
        qz_copy(i).start()

    def keep_own(p, carry):
        own[p] = partial(p, y)
        return carry

    lax.fori_loop(0, moments, keep_own, 0)

    for i in range(1, zc):
        qz_copy(i).wait_recv()
    total = q_z[...].astype(F32)
    for i in range(1, zc):
        total = total + q_zr[i - 1].astype(F32)
    q_f[...] = total.astype(BF16)
    qf_copy().start()

    def scatter(p):
        y_copy(p).wait_recv()
        summed = (own[p] + yrecv[p].astype(F32)).astype(BF16)
        for c in range(zc):
            for part in range(2):
                first = part * half + c * chunk
                zsend[p, c, part] = summed[first:first + chunk]
        for i in range(1, zc):
            z_copy(p, i).start()

    def finish(p):
        coef = zsend[p, z].astype(F32)
        for i in range(1, zc):
            z_copy(p, i).wait_recv()
            coef = coef + zrecv[p, i - 1].astype(F32)
        coef = coef.astype(BF16)
        cr, ci = coef[0], coef[1]
        left = dot(
            jnp.concatenate(
                [jnp.concatenate([cr, ci], 1), jnp.concatenate([-ci, cr], 1)], 0),
            meson[p]).astype(BF16)
        lr, li = left[:chunk], left[chunk:]
        pair = dot(
            jnp.concatenate(
                [jnp.concatenate([lr, -li], 1), jnp.concatenate([li, lr], 1)], 0),
            zfull[...])
        for owner in range(tc):
            for part in range(2):
                first = part * chunk + owner * cl
                osend[p, owner, part] = pair[first:first + cl].astype(BF16)
        for i in range(1, tc):
            x_copy(p, i).start()

    scatter(0)

    qf_copy().wait_recv()
    j_low = lax.broadcasted_iota(jnp.int32, (vecs, small), 1) * NDIL
    k_low = lax.broadcasted_iota(jnp.int32, (vecs, small), 0)
    spread = ((k_low >= j_low) & (k_low < j_low + NDIL)).astype(F32).astype(BF16)

    def widen(values):
        return jnp.where(keep, dot(spread, values), 0.0).astype(BF16)

    zfull[pl.ds(pl.multiple_of(y * vecs, vecs), vecs), :] = widen(q_f[...])
    zfull[pl.ds(pl.multiple_of((1 - y) * vecs, vecs), vecs), :] = widen(q_fr[...])
    meson_copy.wait()

    def step(p, carry):
        scatter(p)
        finish(p - 1)
        return carry

    lax.fori_loop(1, moments, step, 0)
    finish(moments - 1)

    qy_copy().wait_send()
    qf_copy().wait_send()
    for i in range(1, zc):
        qz_copy(i).wait_send()
    for p in range(moments):
        y_copy(p).wait_send()
        for i in range(1, zc):
            z_copy(p, i).wait_send()
        for i in range(1, tc):
            x_copy(p, i).wait()
    for p in range(moments):
        for owner in range(tc):
            out_ref[p, owner] = xrecv[p, owner]
        out_ref[p, t] = osend[p, t]


def body(solutions, eigvecs, meson, momenta, source_time, dilution):
    times_local, _, colors, sites, cols = solutions.shape
    vecs = eigvecs.shape[4]
    moments = momenta.shape[0]
    sc = lax.axis_size("space")
    tc = lax.axis_size("tm")
    zc = sc // 2
    assert times_local == 1 and sc % 2 == 0
    depth = 2 * colors * sites
    flat = colors * sites
    half = cols // 2
    chunk = cols // sc
    cl = chunk // tc
    small = vecs // NDIL

    space = lax.axis_index("space")
    site = space * sites + jnp.arange(sites, dtype=jnp.int32)
    coordinates = jnp.stack([site % SIDE, site // SIDE % SIDE, site // (SIDE * SIDE)], 0)
    windings = jnp.sum(momenta[:, :, None] * coordinates[None], 1)
    angles = 2.0 * jnp.pi / SIDE * windings.astype(F32)
    angles = jnp.tile(angles, (1, colors))[:, None, :]

    column = np.arange(cols)
    owner, within = column // cl, column % cl
    o_t, o_s = owner // sc, owner % sc
    dst = (((o_s % 2) * zc + o_s // 2) * tc + o_t) * cl + within

    vm = pl.BlockSpec(memory_space=pltpu.VMEM)
    dma = pltpu.SemaphoreType.DMA
    nz, nt = max(zc - 1, 1), max(tc - 1, 1)
    received = pl.pallas_call(
        functools.partial(kernel, zc, tc),
        out_shape=jax.ShapeDtypeStruct((moments, tc, 2, cl, cols), BF16),
        in_specs=[vm, vm, pl.BlockSpec(memory_space=pl.ANY), vm, vm, vm, vm],
        out_specs=vm,
        scratch_shapes=[
            pltpu.VMEM((moments, 2 * vecs, vecs), BF16),
            pltpu.VMEM((2, half, depth), F32),
            pltpu.VMEM((cols, depth), BF16),
            pltpu.VMEM((moments, cols, vecs), BF16),
            pltpu.VMEM((moments, cols, vecs), BF16),
            pltpu.VMEM((moments, cols, vecs), F32),
            pltpu.VMEM((moments, zc, 2, chunk, vecs), BF16),
            pltpu.VMEM((moments, nz, 2, chunk, vecs), BF16),
            pltpu.VMEM((moments, tc, 2, cl, cols), BF16),
            pltpu.VMEM((2, small, cols), BF16),
            pltpu.VMEM((small, cols), BF16),
            pltpu.VMEM((small, cols), BF16),
            pltpu.VMEM((nz, small, cols), BF16),
            pltpu.VMEM((small, cols), BF16),
            pltpu.VMEM((small, cols), BF16),
            pltpu.VMEM((2 * vecs, cols), BF16),
            pltpu.VMEM((moments, tc, 2, cl, cols), BF16),
            dma, dma((moments,)), dma((moments,)),
            dma((moments, nz)), dma((moments, nz)),
            dma((moments, nt)), dma((moments, nt)),
            dma, dma, dma((nz,)), dma((nz,)), dma, dma,
        ],
        compiler_params=pltpu.CompilerParams(
            collective_id=0, has_side_effects=True, vmem_limit_bytes=48 * 1024 * 1024),
    )(
        solutions.reshape(depth, cols),
        eigvecs.reshape(depth, vecs),
        meson.reshape(moments, 2 * vecs, vecs),
        jnp.cos(angles),
        jnp.sin(angles),
        jnp.asarray(dst[None, :], jnp.int32),
        dilution[None, :],
    )

    first = (lax.axis_index("tm") * sc + space) * cl
    mine = lax.dynamic_slice_in_dim(source_time, first, cl)
    wanted = (mine[:, None] + jnp.arange(tc, dtype=jnp.int32)[None, :]) % tc
    wanted = wanted[None, None, :, :, None]
    result = jnp.zeros((moments, 2, cl, tc, cols), F32)
    for time in range(tc):
        result = jnp.where(wanted == time, received[:, time, :, :, None, :].astype(F32), result)
    return result


def solution(mesh):
    return jax.shard_map(
        body,
        mesh=mesh,
        in_specs=(
            P(("cfg", "tm"), None, None, "space", None),
            P(("cfg", "tm"), None, None, "space", None),
            P(None, ("cfg", "tm"), None, None, None),
            P(),
            P(),
            P(),
        ),
        out_specs=P(None, None, ("tm", "space"), "cfg", None),
        check_vma=False,
    )
```

time: 182 us -> 68.1 us (0.37)
  blocking collectives: 92.2 us -> 0 us
  Pallas kernels: 0 us -> 59.4 us
  waiting for transfers between devices: 30.5 us -> 0 us
  local copies, waits for them, and re-layouts: 22.2 us -> 6.7 us
  between operations: 13.7 us -> 0.07 us
  matrix products: 11.9 us -> 0 us
  other arithmetic: 7.73 us -> 1.63 us
  starting transfers between devices: 3.63 us -> 0 us
    psum x1 -> x0, blocking collectives: 92.2 us -> none  [body(): zero_all = lax.psum(zero_terms, 'space').astype(jnp.bfloat16)[:, :, 0]]
    pallas_call x0 -> x1, Pallas kernels: none -> 59.4 us  [body(): pl.pallas_call(functools.partial(kernel, zc, tc), out_shape=jax.ShapeDtyp...]
    reduce_scatter x1 -> x0, waiting for transfers between devices: 25.2 us -> none  [body(): lax.psum_scatter(project(phased_real, phased_imag, vec_real, vec_imag, mo...]
    another operation x7 -> x0, local copies, waits for them, and re-layouts: 12.9 us -> none  [the longest x4 9.73 us: project(): stacked = jnp.stack([real_part, imag_part], 2)]
    dot_general x17 -> x0, matrix products: 11.9 us -> none  [the longest x8 9.17 us: contract(): lax.dot_general(first_op, second_op, (((1,), (1,)), ((0,), (0,))), prefer...]
    all_to_all x1 -> x0, waiting for transfers between devices: 5.24 us -> none  [body(): lax.all_to_all(outgoing.astype(jnp.bfloat16), 'tm', split_axis=1, concat_...]
    all_to_all x1 -> x0, starting transfers between devices: 3.63 us -> none  [body(): lax.all_to_all(outgoing.astype(jnp.bfloat16), 'tm', split_axis=1, concat_...]
    convert_element_type x3 -> x1, other arithmetic: 3.63 us -> 0.04 us  [body(): received[:, time, :, :, None, :].astype(F32)]
  transfers between devices with their start and end apart: 2 -> 0, of which waited for: 2 -> 0; matrix products, arithmetic and copies ran while one was open for 3% -> 0% of each run, Pallas kernels for 0% -> 0%
where the time goes in v1:
time: 68.1 us; the launch traced here: 67.8 us
  Pallas kernels  59.4 us (87%)
  local copies, waits for them, and re-layouts  6.7 us (10%)
  other arithmetic  1.63 us (2%)
    pallas_call x1, Pallas kernels, body(): pl.pallas_call(functools.partial(kernel, zc, tc), out_shape=jax.ShapeDtyp...  59.4 us
    unnamed x9, local copies, waits for them, and re-layouts  5.23 us

profile of v1, /device:TPU:0, one launch (start us, length us, event | category | flops | bytes accessed | tf_op | source)
XLA Modules:
  0.0 67.8 jit_solution(1245033500659489026)
XLA Ops:
  0.0 0.8 %dynamic_slice.3 = s32[24]{0:T(128)S(1)} dynamic-slice(s32[384]{0:T(512)} %param.11, s32[]{:T(128)S(6)} %select_n.70), dynamic_slice_sizes={24} | dynamic-slice | bytes 196 | tf_op jit(solution)/shard_map/dynamic_slice | solution.py:295
  0.8 0.7 %broadcast_in_dim.38.dil_ref = s32[1,384]{1,0:T(1,128)S(1)} reshape(s32[384]{0:T(512)} %param.12) | data formatting | bytes 3072 | tf_op jit(solution)/shard_map/broadcast_in_dim | solution.py:291
  1.5 0.8 %copy.10 = s32[4,3]{0,1:T(4,128)S(1)} copy(s32[4,3]{1,0:T(4,128)} %param.10) | data formatting | bytes 96 | tf_op args[3]
  2.3 0.1 multiply_reduce_fusion
  2.4 0.1 broadcast_compare_fusion
  2.5 0.0 copy-start
  2.5 1.7 %copy-done = bf16[4,1,2,384,384]{4,3,2,1,0:T(8,128)(2,1)S(1)} copy-done((bf16[4,1,2,384,384]{4,3,2,1,0:T(8,128)(2,1)S(1)}, bf16[4,1,2,384,384]{4,3,2,1,0:T(8,128)(2,1)}, u32[]{:S(2)}) %copy-start) | copy-done | bytes 2359320
  4.2 0.0 copy-start.1
  4.2 1.1 %copy-done.1 = bf16[1,2,3,128,384]{4,3,2,1,0:T(8,128)(2,1)S(1)} copy-done((bf16[1,2,3,128,384]{4,3,2,1,0:T(8,128)(2,1)S(1)}, bf16[1,2,3,128,384]{4,3,2,1,0:T(8,128)(2,1)}, u32[]{:S(2)}) %copy-start.1) | copy-done | bytes 589848
  5.3 0.0 copy-start.2
  5.3 1.1 %copy-done.2 = bf16[1,2,3,128,384]{4,3,2,1,0:T(8,128)(2,1)S(1)} copy-done((bf16[1,2,3,128,384]{4,3,2,1,0:T(8,128)(2,1)S(1)}, bf16[1,2,3,128,384]{4,3,2,1,0:T(8,128)(2,1)}, u32[]{:S(2)}) %copy-start.2) | copy-done | bytes 589848
  6.3 0.0 copy-start.3
  6.3 0.7 %copy-done.3 = s32[1,384]{1,0:T(1,128)S(1)} copy-done((s32[1,384]{1,0:T(1,128)S(1)}, s32[1,384]{1,0:T(1,128)}, u32[]{:S(2)}) %copy-start.3) | copy-done | bytes 1560
  7.0 59.4 %shard_map.73 = bf16[4,2,2,24,384]{4,3,2,1,0:T(8,128)(2,1)S(1)} custom-call(bf16[768,384]{1,0:T(8,128)(2,1)S(1)} %bitcast.14, bf16[768,384]{1,0:T(8,128)(2,1)S(1)} %bitcast.15, bf16[4,768,384]{2,1,0:T(8,128)(2,1)S(1)} %bitcast.13, f32[4,1,384]{2,1,0:T(1,128)S(1)} %copy.11.cos_ref, f32[4,1,384]{2,1,0:T(1,128)S(1)} %copy.12.sin_ref, s32[1,384]{1,0:T(1,128)S(1)} %copy-done.3, ...), custom_call_target="tpu_custom_call" | custom-call | tf_op jit(solution)/shard_map/pallas_call | solution.py:254
  66.5 1.3 %select_select_fusion = f32[4,2,24,2,384]{4,3,2,1,0:T(2,128)} fusion(pred[24,2]{1,0:T(8,128)(4,1)S(1)} %get-tuple-element.10, pred[24,2]{1,0:T(8,128)(4,1)S(1)} %get-tuple-element.9, f32[4,2,24,384]{3,2,1,0:T(8,128)S(1)} %get-tuple-element.6, f32[4,2,24,384]{3,2,1,0:T(8,128)S(1)} %get-tuple-element.5), kind=kLoop, calls=%fused_computation | loop fusion | flops 294912 | bytes 1179744 | tf_op jit(solution)/shard_map/jit(_where)/select_n | solution.py:300
  (9 shorter events, 0.2 us)
Async XLA Ops:
  2.5 1.7 %copy-start = (bf16[4,1,2,384,384]{4,3,2,1,0:T(8,128)(2,1)S(1)}, bf16[4,1,2,384,384]{4,3,2,1,0:T(8,128)(2,1)}, u32[]{:S(2)}) copy-start(bf16[4,1,2,384,384]{4,3,2,1,0:T(8,128)(2,1)} %param.9) | copy-start | bytes 7077892
  4.2 1.1 %copy-start.1 = (bf16[1,2,3,128,384]{4,3,2,1,0:T(8,128)(2,1)S(1)}, bf16[1,2,3,128,384]{4,3,2,1,0:T(8,128)(2,1)}, u32[]{:S(2)}) copy-start(bf16[1,2,3,128,384]{4,3,2,1,0:T(8,128)(2,1)} %param.7) | copy-start | bytes 1769476
  5.3 1.1 %copy-start.2 = (bf16[1,2,3,128,384]{4,3,2,1,0:T(8,128)(2,1)S(1)}, bf16[1,2,3,128,384]{4,3,2,1,0:T(8,128)(2,1)}, u32[]{:S(2)}) copy-start(bf16[1,2,3,128,384]{4,3,2,1,0:T(8,128)(2,1)} %param.8) | copy-start | bytes 1769476
  6.3 0.7 %copy-start.3 = (s32[1,384]{1,0:T(1,128)S(1)}, s32[1,384]{1,0:T(1,128)}, u32[]{:S(2)}) copy-start(s32[1,384]{1,0:T(1,128)} %constant.68.clone.dst_ref) | copy-start | bytes 4612

commit v2 on v1

--- a/solution.py
+++ b/solution.py
@@ -19,17 +19,22 @@
     return lax.dot_general(a, b, (dims, ((), ())), preferred_element_type=F32)
 
 
+def split(values):
+    high = values.astype(BF16)
+    return high, (values - high.astype(F32)).astype(BF16)
+
+
 def kernel(
     zc, tc,
-    sol_ref, eig_ref, meson_hbm, cos_ref, sin_ref, dst_ref, dil_ref,
+    sol_hbm, eig_hbm, meson_hbm, mom_ref, place_ref, dst_ref, dil_ref,
     out_ref,
-    meson, solt, lhs, ysend, yrecv, own, zsend, zrecv, osend,
-    q_y, q_yr, q_z, q_zr, q_f, q_fr, zfull, xrecv,
-    meson_sem, ys, yr, zs, zr, xs, xr, qys, qyr, qzs, qzr, qfs, qfr,
+    sol_ref, eig_ref, meson, cos_ref, sin_ref, solt, lhs, ysend, yrecv, own, ysum, zsend, zrecv, osend,
+    q_own, q_sum, q_y, q_yr, q_z, q_zr, q_f, q_fr, zfull, xrecv,
+    sol_sem, eig_sem, meson_sem, ys, yr, zs, zr, xs, xr, qys, qyr, qzs, qzr, qfs, qfr,
 ):
-    moments = cos_ref.shape[0]
-    depth, cols = sol_ref.shape
-    vecs = eig_ref.shape[1]
+    moments = mom_ref.shape[0]
+    depth, cols = sol_hbm.shape
+    vecs = eig_hbm.shape[1]
     half = cols // 2
     flat = depth // 2
     chunk = half // zc
@@ -80,6 +85,10 @@
             src_ref=q_f, dst_ref=q_fr, send_sem=qfs, recv_sem=qfr,
             device_id=ypeer, device_id_type=MESH)
 
+    sol_copy = pltpu.make_async_copy(sol_hbm, sol_ref, sol_sem)
+    sol_copy.start()
+    eig_copy = pltpu.make_async_copy(eig_hbm, eig_ref, eig_sem)
+    eig_copy.start()
     meson_copy = pltpu.make_async_copy(meson_hbm, meson, meson_sem)
     meson_copy.start()
 
@@ -90,18 +99,32 @@
     for i in range(1, tc):
         pl.semaphore_signal(barrier, inc=1, device_id={"tm": xpeer(i)}, device_id_type=MESH)
 
+    colors = flat // place_ref.shape[2]
+    places = place_ref[s]
+    for p in range(moments):
+        winding = mom_ref[p, 0] * places[0:1]
+        for axis in range(1, 3):
+            winding = winding + mom_ref[p, axis] * places[axis:axis + 1]
+        angle = 2.0 * jnp.pi / SIDE * winding.astype(F32)
+        cos_ref[p] = jnp.concatenate([jnp.cos(angle)] * colors, 1)
+        sin_ref[p] = jnp.concatenate([jnp.sin(angle)] * colors, 1)
+
+    sol_copy.wait()
+    eig_copy.wait()
     sol = sol_ref[...]
     eig = eig_ref[...]
     turned = jnp.concatenate([sol[flat:], -sol[:flat]], 0)
     k_row = lax.broadcasted_iota(jnp.int32, (vecs, cols), 0)
-    keep = (k_row & (NDIL - 1)) == dil_ref[...]
+    keep = (k_row & (NDIL - 1)) == dil_ref[...].reshape(1, cols)
     j_row = lax.broadcasted_iota(jnp.int32, (small, vecs), 0) * NDIL
     k_col = lax.broadcasted_iota(jnp.int32, (small, vecs), 1)
     gather = ((k_col >= j_row) & (k_col < j_row + NDIL)).astype(F32).astype(BF16)
     for part, rhs in enumerate((sol, turned)):
         full = dot(eig, rhs, ((0,), (0,)))
-        full = jnp.where(keep, full, 0.0).astype(BF16)
-        q_y[part] = dot(gather, full).astype(BF16)
+        high, low = split(jnp.where(keep, full, 0.0))
+        packed = dot(gather, high) + dot(gather, low)
+        q_own[part] = packed
+        q_y[part] = packed.astype(BF16)
 
     c_row = lax.broadcasted_iota(jnp.int32, (cols, cols), 0)
     perm = (c_row == dst_ref[...]).astype(F32).astype(BF16)
@@ -132,7 +155,8 @@
     lax.fori_loop(0, moments, send_other, 0)
 
     qy_copy().wait_recv()
-    q_z[...] = (q_y[y].astype(F32) + q_yr[...].astype(F32)).astype(BF16)
+    q_sum[...] = q_own[y] + q_yr[...].astype(F32)
+    q_z[...] = q_sum[...].astype(BF16)
     for i in range(1, zc):
         qz_copy(i).start()
 
@@ -144,7 +168,7 @@
 
     for i in range(1, zc):
         qz_copy(i).wait_recv()
-    total = q_z[...].astype(F32)
+    total = q_sum[...]
     for i in range(1, zc):
         total = total + q_zr[i - 1].astype(F32)
     q_f[...] = total.astype(BF16)
@@ -152,30 +176,31 @@
 
     def scatter(p):
         y_copy(p).wait_recv()
-        summed = (own[p] + yrecv[p].astype(F32)).astype(BF16)
         for c in range(zc):
             for part in range(2):
-                first = part * half + c * chunk
-                zsend[p, c, part] = summed[first:first + chunk]
+                rows = pl.ds(part * half + c * chunk, chunk)
+                summed = own[p, rows] + yrecv[p, rows].astype(F32)
+                ysum[p, c, part] = summed
+                zsend[p, c, part] = summed.astype(BF16)
         for i in range(1, zc):
             z_copy(p, i).start()
 
     def finish(p):
-        coef = zsend[p, z].astype(F32)
+        coef = ysum[p, z]
         for i in range(1, zc):
             z_copy(p, i).wait_recv()
             coef = coef + zrecv[p, i - 1].astype(F32)
-        coef = coef.astype(BF16)
         cr, ci = coef[0], coef[1]
-        left = dot(
-            jnp.concatenate(
-                [jnp.concatenate([cr, ci], 1), jnp.concatenate([-ci, cr], 1)], 0),
-            meson[p]).astype(BF16)
+        rows = 2 * chunk
+        both = split(jnp.concatenate(
+            [jnp.concatenate([cr, ci], 1), jnp.concatenate([-ci, cr], 1)], 0))
+        left = dot(jnp.concatenate(both, 0), meson[p])
+        left = left[:rows] + left[rows:]
         lr, li = left[:chunk], left[chunk:]
-        pair = dot(
-            jnp.concatenate(
-                [jnp.concatenate([lr, -li], 1), jnp.concatenate([li, lr], 1)], 0),
-            zfull[...])
+        both = split(jnp.concatenate(
+            [jnp.concatenate([lr, -li], 1), jnp.concatenate([li, lr], 1)], 0))
+        pair = dot(jnp.concatenate(both, 0), zfull[...])
+        pair = pair[:rows] + pair[rows:]
         for owner in range(tc):
             for part in range(2):
                 first = part * chunk + owner * cl
@@ -237,11 +262,8 @@
     small = vecs // NDIL
 
     space = lax.axis_index("space")
-    site = space * sites + jnp.arange(sites, dtype=jnp.int32)
-    coordinates = jnp.stack([site % SIDE, site // SIDE % SIDE, site // (SIDE * SIDE)], 0)
-    windings = jnp.sum(momenta[:, :, None] * coordinates[None], 1)
-    angles = 2.0 * jnp.pi / SIDE * windings.astype(F32)
-    angles = jnp.tile(angles, (1, colors))[:, None, :]
+    site = np.arange(sc * sites).reshape(sc, 1, sites)
+    places = np.concatenate([site % SIDE, site // SIDE % SIDE, site // (SIDE * SIDE)], 1)
 
     column = np.arange(cols)
     owner, within = column // cl, column % cl
@@ -249,23 +271,31 @@
     dst = (((o_s % 2) * zc + o_s // 2) * tc + o_t) * cl + within
 
     vm = pl.BlockSpec(memory_space=pltpu.VMEM)
+    hbm = pl.BlockSpec(memory_space=pltpu.HBM)
     dma = pltpu.SemaphoreType.DMA
     nz, nt = max(zc - 1, 1), max(tc - 1, 1)
     received = pl.pallas_call(
         functools.partial(kernel, zc, tc),
         out_shape=jax.ShapeDtypeStruct((moments, tc, 2, cl, cols), BF16),
-        in_specs=[vm, vm, pl.BlockSpec(memory_space=pl.ANY), vm, vm, vm, vm],
+        in_specs=[hbm, hbm, hbm, pl.BlockSpec(memory_space=pltpu.SMEM), vm, vm, vm],
         out_specs=vm,
         scratch_shapes=[
+            pltpu.VMEM((depth, cols), BF16),
+            pltpu.VMEM((depth, vecs), BF16),
             pltpu.VMEM((moments, 2 * vecs, vecs), BF16),
+            pltpu.VMEM((moments, 1, flat), F32),
+            pltpu.VMEM((moments, 1, flat), F32),
             pltpu.VMEM((2, half, depth), F32),
             pltpu.VMEM((cols, depth), BF16),
             pltpu.VMEM((moments, cols, vecs), BF16),
             pltpu.VMEM((moments, cols, vecs), BF16),
             pltpu.VMEM((moments, cols, vecs), F32),
+            pltpu.VMEM((moments, zc, 2, chunk, vecs), F32),
             pltpu.VMEM((moments, zc, 2, chunk, vecs), BF16),
             pltpu.VMEM((moments, nz, 2, chunk, vecs), BF16),
             pltpu.VMEM((moments, tc, 2, cl, cols), BF16),
+            pltpu.VMEM((2, small, cols), F32),
+            pltpu.VMEM((small, cols), F32),
             pltpu.VMEM((2, small, cols), BF16),
             pltpu.VMEM((small, cols), BF16),
             pltpu.VMEM((small, cols), BF16),
@@ -274,21 +304,21 @@
             pltpu.VMEM((small, cols), BF16),
             pltpu.VMEM((2 * vecs, cols), BF16),
             pltpu.VMEM((moments, tc, 2, cl, cols), BF16),
-            dma, dma((moments,)), dma((moments,)),
+            dma, dma, dma, dma((moments,)), dma((moments,)),
             dma((moments, nz)), dma((moments, nz)),
             dma((moments, nt)), dma((moments, nt)),
             dma, dma, dma((nz,)), dma((nz,)), dma, dma,
         ],
         compiler_params=pltpu.CompilerParams(
-            collective_id=0, has_side_effects=True, vmem_limit_bytes=48 * 1024 * 1024),
+            collective_id=0, has_side_effects=True),
     )(
         solutions.reshape(depth, cols),
         eigvecs.reshape(depth, vecs),
         meson.reshape(moments, 2 * vecs, vecs),
-        jnp.cos(angles),
-        jnp.sin(angles),
+        momenta,
+        jnp.asarray(places, jnp.int32),
         jnp.asarray(dst[None, :], jnp.int32),
-        dilution[None, :],
+        dilution,
     )
 
     first = (lax.axis_index("tm") * sc + space) * cl

time: 68.1 us -> 65.8 us (0.966)
  local copies, waits for them, and re-layouts: 6.7 us -> 0.75 us
  Pallas kernels: 59.4 us -> 62.4 us
  other arithmetic: 1.63 us -> 2.44 us
    unnamed x9 -> x0, local copies, waits for them, and re-layouts: 5.23 us -> none
    pallas_call x1, Pallas kernels: 59.4 us -> 62.4 us  [body(): pl.pallas_call(functools.partial(kernel, zc, tc), out_shape=jax.ShapeDtyp...]
    convert_element_type x1, other arithmetic: 0.04 us -> 1.03 us  [body(): received[:, time, :, :, None, :].astype(F32)]
    broadcast_in_dim x1 -> x0, local copies, waits for them, and re-layouts: 0.69 us -> none  [body(): dilution[None, :]]
where the time goes in v2:
time: 65.8 us; the launch traced here: 65.6 us
  Pallas kernels  62.4 us (95%)
  other arithmetic  2.44 us (4%)
  local copies, waits for them, and re-layouts  0.75 us (1%)
    pallas_call x1, Pallas kernels, body(): pl.pallas_call(functools.partial(kernel, zc, tc), out_shape=jax.ShapeDtyp...  62.4 us
    select_n x1, other arithmetic, body(): jnp.where(wanted == time, received[:, time, :, :, None, :].astype(F32), r...  1.32 us

profile of v2, /device:TPU:0, one launch (start us, length us, event | category | flops | bytes accessed | tf_op | source)
XLA Modules:
  0.0 65.6 jit_solution(16876613310858674563)
XLA Ops:
  0.0 0.8 %dynamic_slice.3 = s32[24]{0:T(128)S(1)} dynamic-slice(s32[384]{0:T(512)} %param.12, s32[]{:T(128)S(6)} %select_n.24), dynamic_slice_sizes={24} | dynamic-slice | bytes 196 | tf_op jit(solution)/shard_map/dynamic_slice | solution.py:325
  0.8 0.1 broadcast_compare_fusion
  0.8 62.4 %shard_map.82 = bf16[4,2,2,24,384]{4,3,2,1,0:T(8,128)(2,1)} custom-call(bf16[768,384]{1,0:T(8,128)(2,1)} %bitcast.10, bf16[768,384]{1,0:T(8,128)(2,1)} %bitcast.11, bf16[4,768,384]{2,1,0:T(8,128)(2,1)} %bitcast.9, s32[4,3]{1,0:T(4,128)} %mom_ref.1, s32[8,3,128]{2,1,0:T(4,128)} %constant.39.clone.place_ref, s32[1,384]{1,0:T(1,128)} %constant.40.clone.dst_ref, ...), custom_call_target="tpu_custom_call" | custom-call | tf_op jit(solution)/shard_map/pallas_call | solution.py:277
  63.2 1.0 %bitcast_convert_fusion.1 = (f32[4,2,24,384]{3,2,1,0:T(8,128)S(1)}, f32[4,2,24,384]{3,2,1,0:T(8,128)S(1)}) fusion(bf16[4,2,2,24,384]{4,3,2,1,0:T(8,128)(2,1)} %shard_map.82), kind=kLoop, calls=%fused_computation.2 | loop fusion | flops 147456 | bytes 884736 | tf_op jit(solution)/shard_map/convert_element_type | solution.py:330
  64.3 1.3 %select_select_fusion = f32[4,2,24,2,384]{4,3,2,1,0:T(2,128)} fusion(pred[24,2]{1,0:T(8,128)(4,1)S(1)} %get-tuple-element.8, pred[24,2]{1,0:T(8,128)(4,1)S(1)} %get-tuple-element.7, f32[4,2,24,384]{3,2,1,0:T(8,128)S(1)} %get-tuple-element.6, f32[4,2,24,384]{3,2,1,0:T(8,128)S(1)} %get-tuple-element.5), kind=kLoop, calls=%fused_computation | loop fusion | flops 294912 | bytes 1179744 | tf_op jit(solution)/shard_map/jit(_where)/select_n | solution.py:330

commit v3 on v2

v3 whole, which is shorter than its diff:
```python
import functools

import jax
import jax.numpy as jnp
import numpy as np
from jax import lax
from jax.experimental import pallas as pl
from jax.experimental.pallas import tpu as pltpu
from jax.sharding import PartitionSpec as P

SIDE = 48
NDIL = 4
MESH = pl.DeviceIdType.MESH
F32 = jnp.float32
BF16 = jnp.bfloat16


def dot(a, b, dims=((1,), (0,))):
    return lax.dot_general(a, b, (dims, ((), ())), preferred_element_type=F32)


def split(values):
    high = values.astype(BF16)
    return high, (values - high.astype(F32)).astype(BF16)


def kernel(
    zc, tc,
    sol_hbm, eig_hbm, meson_hbm, mom_ref, place_ref, dst_ref, dil_ref,
    out_ref,
    sol_ref, eig_ref, meson, cos_ref, sin_ref, solt, lhs, ysend, yrecv, own,
    ysum, zsend, zrecv, osend, xrecv,
    q_own, q_sum, q_y, q_yr, q_z, q_zr, q_f, q_fr, zfull,
    sol_sem, eig_sem, meson_sem, ys, yr, zs, zr, xs, xr,
    qys, qyr, qzs, qzr, qas, qar, qfs, qfr,
):
    moments = mom_ref.shape[0]
    depth, cols = sol_hbm.shape
    vecs = eig_hbm.shape[1]
    flat = depth // 2
    pieces = 2 * moments
    low_count = tc // 2
    cl = cols // (2 * zc * tc)
    sub = low_count * cl
    prow = zc * sub
    small = vecs // NDIL
    q_rows = small // zc

    s = lax.axis_index("space")
    t = lax.axis_index("tm")
    y = s % 2
    z = s // 2
    group = t // low_count
    low = t % low_count
    ypeer = {"space": z * 2 + (1 - y)}

    def zpeer(i):
        return {"space": ((z + i) % zc) * 2 + y}

    def y_copy(n):
        return pltpu.make_async_remote_copy(
            src_ref=ysend.at[n], dst_ref=yrecv.at[n], send_sem=ys.at[n], recv_sem=yr.at[n],
            device_id=ypeer, device_id_type=MESH)

    def z_copy(n, i):
        return pltpu.make_async_remote_copy(
            src_ref=zsend.at[n, (z + i) % zc], dst_ref=zrecv.at[n, i - 1],
            send_sem=zs.at[n, i - 1], recv_sem=zr.at[n, i - 1],
            device_id=zpeer(i), device_id_type=MESH)

    def x_copy(p, cross, i):
        side = 1 - group if cross else group
        peer = side * low_count + (low + i) % low_count
        slot = i if cross else low_count + i
        return pltpu.make_async_remote_copy(
            src_ref=osend.at[p, peer], dst_ref=xrecv.at[p, t],
            send_sem=xs.at[p, slot], recv_sem=xr.at[p, slot],
            device_id={"tm": peer}, device_id_type=MESH)

    def qy_copy():
        return pltpu.make_async_remote_copy(
            src_ref=q_y.at[1 - y], dst_ref=q_yr, send_sem=qys, recv_sem=qyr,
            device_id=ypeer, device_id_type=MESH)

    def qz_copy(i):
        return pltpu.make_async_remote_copy(
            src_ref=q_z.at[(z + i) % zc], dst_ref=q_zr.at[i - 1],
            send_sem=qzs.at[i - 1], recv_sem=qzr.at[i - 1],
            device_id=zpeer(i), device_id_type=MESH)

    def qa_copy(i):
        return pltpu.make_async_remote_copy(
            src_ref=q_f.at[z], dst_ref=q_f.at[z],
            send_sem=qas.at[i - 1], recv_sem=qar.at[i - 1],
            device_id=zpeer(i), device_id_type=MESH)

    def qf_copy():
        return pltpu.make_async_remote_copy(
            src_ref=q_f, dst_ref=q_fr, send_sem=qfs, recv_sem=qfr,
            device_id=ypeer, device_id_type=MESH)

    sol_copy = pltpu.make_async_copy(sol_hbm, sol_ref, sol_sem)
    sol_copy.start()
    eig_copy = pltpu.make_async_copy(eig_hbm, eig_ref, eig_sem)
    eig_copy.start()
    meson_copy = pltpu.make_async_copy(meson_hbm, meson, meson_sem)
    meson_copy.start()

    barrier = pltpu.get_barrier_semaphore()
    pl.semaphore_signal(barrier, inc=1, device_id=ypeer, device_id_type=MESH)
    for i in range(1, zc):
        pl.semaphore_signal(barrier, inc=1, device_id=zpeer(i), device_id_type=MESH)
    for i in range(1, tc):
        pl.semaphore_signal(
            barrier, inc=1, device_id={"tm": (t + i) % tc}, device_id_type=MESH)

    colors = flat // place_ref.shape[2]
    places = place_ref[s]
    for p in range(moments):
        winding = mom_ref[p, 0] * places[0:1]
        for axis in range(1, 3):
            winding = winding + mom_ref[p, axis] * places[axis:axis + 1]
        angle = 2.0 * jnp.pi / SIDE * winding.astype(F32)
        cos_ref[p] = jnp.concatenate([jnp.cos(angle)] * colors, 1)
        sin_ref[p] = jnp.concatenate([jnp.sin(angle)] * colors, 1)

    c_row = lax.broadcasted_iota(jnp.int32, (cols, cols), 0)
    perm = (c_row == dst_ref[...]).astype(F32).astype(BF16)
    sol_copy.wait()
    moved = dot(perm, sol_ref[...], ((1,), (1,)))
    for block in range(4):
        solt[block] = moved[block * prow:(block + 1) * prow]
    eig_copy.wait()

    def partial(n, which):
        p = n // 2
        block = solt[which * 2 + (group + 1 + n) % 2]
        re, im = block[:, :flat], block[:, flat:]
        c, sn = cos_ref[p], sin_ref[p]
        pr = (c * re + sn * im).astype(BF16)
        pi = (c * im - sn * re).astype(BF16)
        lhs[:prow, :flat] = pr
        lhs[:prow, flat:] = pi
        lhs[prow:, :flat] = pi
        lhs[prow:, flat:] = -pr
        return dot(lhs[...], eig_ref[...])

    def send_other(n, carry):
        ysend[n] = partial(n, 1 - y).astype(BF16)
        y_copy(n).start()
        return carry

    def keep_own(n, carry):
        own[n] = partial(n, y)
        return carry

    def scatter(n, carry):
        y_copy(n).wait_recv()
        for c in range(zc):
            for part in range(2):
                rows = pl.ds(part * prow + c * sub, sub)
                summed = own[n, rows] + yrecv[n, rows].astype(F32)
                ysum[n, c, part] = summed
                zsend[n, c, part] = summed.astype(BF16)
        for i in range(1, zc):
            z_copy(n, i).start()
        return carry

    def finish(n, carry):
        p = n // 2
        side = (group + 1 + n) % 2
        coef = ysum[n, z]
        for i in range(1, zc):
            z_copy(n, i).wait_recv()
            coef = coef + zrecv[n, i - 1].astype(F32)
        cr, ci = coef[0], coef[1]
        rows = 2 * sub
        both = split(jnp.concatenate(
            [jnp.concatenate([cr, ci], 1), jnp.concatenate([-ci, cr], 1)], 0))
        left = dot(jnp.concatenate(both, 0), meson[p])
        left = left[:rows] + left[rows:]
        lr, li = left[:sub], left[sub:]
        both = split(jnp.concatenate(
            [jnp.concatenate([lr, -li], 1), jnp.concatenate([li, lr], 1)], 0))
        pair = dot(jnp.concatenate(both, 0), zfull[...])
        pair = pair[:rows] + pair[rows:]
        for owner in range(low_count):
            for part in range(2):
                first = part * sub + owner * cl
                osend[p, side * low_count + owner, part] = pair[first:first + cl].astype(BF16)

        @pl.when(n % 2 == 0)
        def _():
            for i in range(low_count):
                x_copy(p, True, i).start()

        if low_count > 1:
            @pl.when(n % 2 == 1)
            def _():
                for i in range(1, low_count):
                    x_copy(p, False, i).start()

        return carry

    def run(stage, first, last):
        lax.fori_loop(first, last, stage, 0)

    pl.semaphore_wait(barrier, 1 + (zc - 1) + (tc - 1))
    run(send_other, 0, 1)

    sol = sol_ref[...]
    eig = eig_ref[...]
    turned = jnp.concatenate([sol[flat:], -sol[:flat]], 0)
    k_row = lax.broadcasted_iota(jnp.int32, (vecs, cols), 0)
    keep = (k_row & (NDIL - 1)) == dil_ref[...].reshape(1, cols)
    j_row = lax.broadcasted_iota(jnp.int32, (small, vecs), 0) * NDIL
    k_col = lax.broadcasted_iota(jnp.int32, (small, vecs), 1)
    gather = ((k_col >= j_row) & (k_col < j_row + NDIL)).astype(F32).astype(BF16)
    for part, rhs in enumerate((sol, turned)):
        full = dot(eig, rhs, ((0,), (0,)))
        high, rest = split(jnp.where(keep, full, 0.0))
        packed = dot(gather, high) + dot(gather, rest)
        q_own[part] = packed
        q_y[part] = packed.astype(BF16)
    qy_copy().start()

    run(send_other, 1, 3)

    qy_copy().wait_recv()
    for c in range(zc):
        rows = pl.ds(c * q_rows, q_rows)
        summed = q_own[y, rows] + q_yr[rows].astype(F32)
        q_sum[c] = summed
        q_z[c] = summed.astype(BF16)
    for i in range(1, zc):
        qz_copy(i).start()

    run(send_other, 3, 5)
    run(keep_own, 0, 2)
    run(scatter, 0, 1)

    for i in range(1, zc):
        qz_copy(i).wait_recv()
    total = q_sum[z]
    for i in range(1, zc):
        total = total + q_zr[i - 1].astype(F32)
    q_f[z] = total.astype(BF16)
    for i in range(1, zc):
        qa_copy(i).start()

    run(keep_own, 2, 4)
    run(scatter, 1, 2)
    for i in range(1, zc):
        qa_copy(i).wait_recv()
    qf_copy().start()

    run(send_other, 5, pieces)
    run(scatter, 2, 3)
    run(keep_own, 4, pieces)
    run(scatter, 3, 4)

    qf_copy().wait_recv()
    j_low = lax.broadcasted_iota(jnp.int32, (vecs, small), 1) * NDIL
    k_low = lax.broadcasted_iota(jnp.int32, (vecs, small), 0)
    spread = ((k_low >= j_low) & (k_low < j_low + NDIL)).astype(F32).astype(BF16)

    def widen(ref):
        values = jnp.concatenate([ref[c].astype(F32) for c in range(zc)], 0).astype(BF16)
        return jnp.where(keep, dot(spread, values), 0.0).astype(BF16)

    zfull[pl.ds(pl.multiple_of(y * vecs, vecs), vecs), :] = widen(q_f)
    zfull[pl.ds(pl.multiple_of((1 - y) * vecs, vecs), vecs), :] = widen(q_fr)
    meson_copy.wait()

    def step(n, carry):
        scatter(n, 0)
        finish(n - 4, 0)
        return carry

    run(step, 4, pieces)
    run(finish, pieces - 4, pieces)

    qy_copy().wait_send()
    qf_copy().wait_send()
    for i in range(1, zc):
        qz_copy(i).wait_send()
        qa_copy(i).wait_send()

    def drain(n, carry):
        y_copy(n).wait_send()
        for i in range(1, zc):
            z_copy(n, i).wait_send()
        return carry

    run(drain, 0, pieces)
    for p in range(moments):
        for i in range(low_count):
            x_copy(p, True, i).wait()
        for i in range(1, low_count):
            x_copy(p, False, i).wait()
        for owner in range(tc):
            out_ref[p, owner] = xrecv[p, owner]
        out_ref[p, t] = osend[p, t]


def body(solutions, eigvecs, meson, momenta, source_time, dilution):
    times_local, _, colors, sites, cols = solutions.shape
    vecs = eigvecs.shape[4]
    moments = momenta.shape[0]
    sc = lax.axis_size("space")
    tc = lax.axis_size("tm")
    zc = sc // 2
    assert times_local == 1 and sc % 2 == 0 and tc % 2 == 0 and moments >= 3
    depth = 2 * colors * sites
    flat = colors * sites
    cl = cols // (sc * tc)
    low_count = tc // 2
    sub = low_count * cl
    prow = zc * sub
    pieces = 2 * moments
    small = vecs // NDIL
    q_rows = small // zc

    space = lax.axis_index("space")
    site = np.arange(sc * sites).reshape(sc, 1, sites)
    places = np.concatenate([site % SIDE, site // SIDE % SIDE, site // (SIDE * SIDE)], 1)

    column = np.arange(cols)
    owner, within = column // cl, column % cl
    o_t, o_s = owner // sc, owner % sc
    block = (o_s % 2) * 2 + o_t // low_count
    dst = ((block * zc + o_s // 2) * low_count + o_t % low_count) * cl + within

    vm = pl.BlockSpec(memory_space=pltpu.VMEM)
    hbm = pl.BlockSpec(memory_space=pltpu.HBM)
    dma = pltpu.SemaphoreType.DMA
    nz = max(zc - 1, 1)
    received = pl.pallas_call(
        functools.partial(kernel, zc, tc),
        out_shape=jax.ShapeDtypeStruct((moments, tc, 2, cl, cols), BF16),
        in_specs=[hbm, hbm, hbm, pl.BlockSpec(memory_space=pltpu.SMEM), vm, vm, vm],
        out_specs=vm,
        scratch_shapes=[
            pltpu.VMEM((depth, cols), BF16),
            pltpu.VMEM((depth, vecs), BF16),
            pltpu.VMEM((moments, 2 * vecs, vecs), BF16),
            pltpu.VMEM((moments, 1, flat), F32),
            pltpu.VMEM((moments, 1, flat), F32),
            pltpu.VMEM((4, prow, depth), F32),
            pltpu.VMEM((2 * prow, depth), BF16),
            pltpu.VMEM((pieces, 2 * prow, vecs), BF16),
            pltpu.VMEM((pieces, 2 * prow, vecs), BF16),
            pltpu.VMEM((pieces, 2 * prow, vecs), F32),
            pltpu.VMEM((pieces, zc, 2, sub, vecs), F32),
            pltpu.VMEM((pieces, zc, 2, sub, vecs), BF16),
            pltpu.VMEM((pieces, nz, 2, sub, vecs), BF16),
            pltpu.VMEM((moments, tc, 2, cl, cols), BF16),
            pltpu.VMEM((moments, tc, 2, cl, cols), BF16),
            pltpu.VMEM((2, small, cols), F32),
            pltpu.VMEM((zc, q_rows, cols), F32),
            pltpu.VMEM((2, small, cols), BF16),
            pltpu.VMEM((small, cols), BF16),
            pltpu.VMEM((zc, q_rows, cols), BF16),
            pltpu.VMEM((nz, q_rows, cols), BF16),
            pltpu.VMEM((zc, q_rows, cols), BF16),
            pltpu.VMEM((zc, q_rows, cols), BF16),
            pltpu.VMEM((2 * vecs, cols), BF16),
            dma, dma, dma,
            dma((pieces,)), dma((pieces,)),
            dma((pieces, nz)), dma((pieces, nz)),
            dma((moments, tc)), dma((moments, tc)),
            dma, dma, dma((nz,)), dma((nz,)), dma((nz,)), dma((nz,)), dma, dma,
        ],
        compiler_params=pltpu.CompilerParams(
            collective_id=0, has_side_effects=True),
    )(
        solutions.reshape(depth, cols),
        eigvecs.reshape(depth, vecs),
        meson.reshape(moments, 2 * vecs, vecs),
        momenta,
        jnp.asarray(places, jnp.int32),
        jnp.asarray(dst[None, :], jnp.int32),
        dilution,
    )

    first = (lax.axis_index("tm") * sc + space) * cl
    mine = lax.dynamic_slice_in_dim(source_time, first, cl)
    wanted = (mine[:, None] + jnp.arange(tc, dtype=jnp.int32)[None, :]) % tc
    wanted = wanted[None, None, :, :, None]
    result = jnp.zeros((moments, 2, cl, tc, cols), F32)
    for time in range(tc):
        result = jnp.where(wanted == time, received[:, time, :, :, None, :].astype(F32), result)
    return result


def solution(mesh):
    return jax.shard_map(
        body,
        mesh=mesh,
        in_specs=(
            P(("cfg", "tm"), None, None, "space", None),
            P(("cfg", "tm"), None, None, "space", None),
            P(None, ("cfg", "tm"), None, None, None),
            P(),
            P(),
            P(),
        ),
        out_specs=P(None, None, ("tm", "space"), "cfg", None),
        check_vma=False,
    )
```

time: 65.8 us -> 50.1 us (0.76)
  Pallas kernels: 62.4 us -> 46.7 us
    pallas_call x1, Pallas kernels: 62.4 us -> 46.7 us  [body(): pl.pallas_call(functools.partial(kernel, zc, tc), out_shape=jax.ShapeDtyp...]
where the time goes in v3:
time: 50.1 us; the launch traced here: 49.9 us
  Pallas kernels  46.7 us (93%)
  other arithmetic  2.44 us (5%)
  local copies, waits for them, and re-layouts  0.75 us (1%)
    pallas_call x1, Pallas kernels, body(): pl.pallas_call(functools.partial(kernel, zc, tc), out_shape=jax.ShapeDtyp...  46.7 us
    select_n x1, other arithmetic, body(): jnp.where(wanted == time, received[:, time, :, :, None, :].astype(F32), r...  1.32 us
    convert_element_type x1, other arithmetic, body(): received[:, time, :, :, None, :].astype(F32)  1.03 us

profile of v3, /device:TPU:0, one launch (start us, length us, event | category | flops | bytes accessed | tf_op | source)
XLA Modules:
  0.0 49.9 jit_solution(7548874325292821263)
XLA Ops:
  0.0 0.8 %dynamic_slice.3 = s32[24]{0:T(128)S(1)} dynamic-slice(s32[384]{0:T(512)} %param.12, s32[]{:T(128)S(6)} %select_n.24), dynamic_slice_sizes={24} | dynamic-slice | bytes 196 | tf_op jit(solution)/shard_map/dynamic_slice | solution.py:387
  0.8 0.1 broadcast_compare_fusion
  0.8 46.7 %shard_map.82 = bf16[4,2,2,24,384]{4,3,2,1,0:T(8,128)(2,1)} custom-call(bf16[768,384]{1,0:T(8,128)(2,1)} %bitcast.10, bf16[768,384]{1,0:T(8,128)(2,1)} %bitcast.11, bf16[4,768,384]{2,1,0:T(8,128)(2,1)} %bitcast.9, s32[4,3]{1,0:T(4,128)} %mom_ref.1, s32[8,3,128]{2,1,0:T(4,128)} %constant.39.clone.place_ref, s32[1,384]{1,0:T(1,128)} %constant.40.clone.dst_ref, ...), custom_call_target="tpu_custom_call" | custom-call | tf_op jit(solution)/shard_map/pallas_call | solution.py:338
  47.6 1.0 %bitcast_convert_fusion.1 = (f32[4,2,24,384]{3,2,1,0:T(8,128)S(1)}, f32[4,2,24,384]{3,2,1,0:T(8,128)S(1)}) fusion(bf16[4,2,2,24,384]{4,3,2,1,0:T(8,128)(2,1)} %shard_map.82), kind=kLoop, calls=%fused_computation.2 | loop fusion | flops 147456 | bytes 884736 | tf_op jit(solution)/shard_map/convert_element_type | solution.py:392
  48.6 1.3 %select_select_fusion = f32[4,2,24,2,384]{4,3,2,1,0:T(2,128)} fusion(pred[24,2]{1,0:T(8,128)(4,1)S(1)} %get-tuple-element.8, pred[24,2]{1,0:T(8,128)(4,1)S(1)} %get-tuple-element.7, f32[4,2,24,384]{3,2,1,0:T(8,128)S(1)} %get-tuple-element.6, f32[4,2,24,384]{3,2,1,0:T(8,128)S(1)} %get-tuple-element.5), kind=kLoop, calls=%fused_computation | loop fusion | flops 294912 | bytes 1179744 | tf_op jit(solution)/shard_map/jit(_where)/select_n | solution.py:392
